TPU v7x, 32 devices: a whole 2x2x4 slice. The times are simulated.
32 devices in a mesh: seq: 8 (over y, x, core), chan: 4 (over z).
Axes of the slice: x: 2, y: 2, z: 4, core: 2. Of those that a mesh axis runs over, the one named last changes fastest.
Arguments:
- hidden_states: bfloat16 [4096, 2048], P('chan', 'seq'), may hold values from -700 to 700
- norm_gain: float32 [4096], P('chan'), may hold values from 0.1 to 1.9
- short_filter: float32 [4096, 128], P('chan'), may hold values from -0.5 to 0.5
- long_filter: bfloat16 [4096, 2048], P('chan', 'seq'), may hold values from -0.125 to 0.125
- long_bias: float32 [4096], P('chan'), may hold values from -4 to 4
- gate_stream: bfloat16 [4096, 2048], P('chan', 'seq'), may hold values from -6 to 6
- upstream: bfloat16 [4096, 2048], P(None, 'seq'), may hold values from -6 to 6
Outputs:
- mixed: bfloat16 [4096, 2048], P('chan', 'seq')
- weight_grad: float32 [4096, 4096], P('seq', 'chan')
All inputs are finite; a program needn't handle non-finite values.
Results may differ from a plain program's by a relative error of at most 0.015.
Values may be sent and summed in bfloat16 or wider, within the bound.
A program may use at most 64 MiB of HBM per device.

v0:
```python
import math
import jax
import jax.numpy as jnp
from jax import lax
from jax.sharding import PartitionSpec as P

D = 4096
EPSILON = 1e-05


def passed_along(value, axis, by):
    devices = lax.axis_size(axis)
    pairs = [(i, i + by) for i in range(devices) if 0 <= i + by < devices]
    return lax.ppermute(value, axis, pairs)


def short_conv(padded, taps):
    kernel = taps[:, ::-1][:, None, :]
    result = lax.conv_general_dilated(
        padded[None],
        kernel,
        (1,),
        "VALID",
        dimension_numbers=("NCH", "OIH", "NCH"),
        feature_group_count=padded.shape[0],
        precision=lax.Precision.HIGHEST,
    )
    return result[0]


def twiddle(row_total, col_total, modulus, direction):
    product = (
        jnp.arange(row_total, dtype=jnp.int32)[:, None]
        * jnp.arange(col_total, dtype=jnp.int32)[None, :]
        % modulus
    )
    angles = direction * 2.0 * math.pi * product.astype(jnp.float32) / modulus
    return (jnp.cos(angles), jnp.sin(angles))


def product_einsum(form, left, right):
    return jnp.einsum(form, left, right, precision=lax.Precision.HIGHEST)


def split_table(table):
    upper = table.astype(jnp.bfloat16)
    lower = (table - upper.astype(jnp.float32)).astype(jnp.bfloat16)
    return (upper, lower)


def table_product(table, grid):
    upper, lower = split_table(table)
    first = jnp.einsum("kn,cnm->ckm", upper, grid, preferred_element_type=jnp.float32)
    return first + jnp.einsum("kn,cnm->ckm", lower, grid, preferred_element_type=jnp.float32)


def forward_real(signal, factor_a, factor_b):
    length = factor_a * factor_b
    seq_total = signal.shape[1]
    kept_in = -(-seq_total // factor_b)
    filled = jnp.pad(signal, ((0, 0), (0, kept_in * factor_b - seq_total)))
    grid = filled.reshape(signal.shape[0], kept_in, factor_b)
    outer_re, outer_im = twiddle(factor_a, kept_in, factor_a, -1.0)
    section_re = table_product(outer_re, grid)
    section_im = table_product(outer_im, grid)
    turn_re, turn_im = twiddle(factor_a, factor_b, length, -1.0)
    rotated_re = section_re * turn_re - section_im * turn_im
    rotated_im = section_re * turn_im + section_im * turn_re
    inner_re, inner_im = twiddle(factor_b, factor_b, factor_b, -1.0)
    result_re = product_einsum("ckm,jm->ckj", rotated_re, inner_re) - product_einsum(
        "ckm,jm->ckj", rotated_im, inner_im
    )
    result_im = product_einsum("ckm,jm->ckj", rotated_re, inner_im) + product_einsum(
        "ckm,jm->ckj", rotated_im, inner_re
    )
    return (result_re, result_im)


def inverse_real(spec_re, spec_im, factor_a, factor_b, kept_rows):
    length = factor_a * factor_b
    inner_re, inner_im = twiddle(factor_b, factor_b, factor_b, 1.0)
    section_re = product_einsum("ckj,mj->ckm", spec_re, inner_re) - product_einsum(
        "ckj,mj->ckm", spec_im, inner_im
    )
    section_im = product_einsum("ckj,mj->ckm", spec_re, inner_im) + product_einsum(
        "ckj,mj->ckm", spec_im, inner_re
    )
    turn_re, turn_im = twiddle(factor_a, factor_b, length, 1.0)
    rotated_re = section_re * turn_re - section_im * turn_im
    rotated_im = section_re * turn_im + section_im * turn_re
    outer_re, outer_im = twiddle(kept_rows, factor_a, factor_a, 1.0)
    result = product_einsum("nk,ckm->cnm", outer_re, rotated_re) - product_einsum(
        "nk,ckm->cnm", outer_im, rotated_im
    )
    return result.reshape(result.shape[0], kept_rows * factor_b) / length


def long_convolution(signal, filt):
    seq_total = signal.shape[1]
    length = 2 * seq_total
    factor_a = 1
    for divisor in range(1, math.isqrt(length) + 1):
        if length % divisor == 0:
            factor_a = divisor
    factor_b = length // factor_a
    signal_re, signal_im = forward_real(signal, factor_a, factor_b)
    filter_re, filter_im = forward_real(filt, factor_a, factor_b)
    joint_re = signal_re * filter_re - signal_im * filter_im
    joint_im = signal_re * filter_im + signal_im * filter_re
    kept_rows = -(-seq_total // factor_b)
    return inverse_real(joint_re, joint_im, factor_a, factor_b, kept_rows)[:, :seq_total]


def shards(hidden_states, norm_gain, short_filter, long_filter, long_bias, gate_stream, upstream):
    states = hidden_states.astype(jnp.float32)
    partial_squares = jnp.sum(states * states, axis=0)
    squares = lax.psum(partial_squares, "chan")
    normed = (states * lax.rsqrt(squares / D + EPSILON)[None, :] * norm_gain[:, None]).astype(
        jnp.bfloat16
    )
    tap_count = short_filter.shape[1]
    width_local = hidden_states.shape[0] // lax.axis_size("seq")
    owner_index = lax.axis_index("seq")
    bias_slice = lax.dynamic_slice_in_dim(long_bias, owner_index * width_local, width_local)
    tail_cols = normed[:, normed.shape[1] - tap_count :]
    from_left = passed_along(tail_cols, "seq", 1)
    padded = jnp.concatenate(
        [from_left[:, 1:].astype(jnp.float32), normed.astype(jnp.float32)], axis=1
    )
    short_out = short_conv(padded, short_filter).astype(jnp.bfloat16)
    short_whole, filter_whole = (
        lax.all_to_all(short_out, "seq", split_axis=0, concat_axis=1, tiled=True),
        lax.all_to_all(long_filter, "seq", split_axis=0, concat_axis=1, tiled=True),
    )
    long_conv = long_convolution(short_whole, filter_whole)
    long_whole = (long_conv + bias_slice[:, None] * short_whole.astype(jnp.float32)).astype(
        jnp.bfloat16
    )
    long_out = lax.all_to_all(long_whole, "seq", split_axis=1, concat_axis=0, tiled=True)
    mixed = (gate_stream.astype(jnp.float32) * long_out.astype(jnp.float32)).astype(jnp.bfloat16)
    mixed_whole = lax.all_gather(mixed, "seq", axis=1, tiled=True)
    owned = lax.all_to_all(upstream, "seq", split_axis=0, concat_axis=1, tiled=True)
    weight_grad = lax.dot_general(
        owned, mixed_whole, (((1,), (1,)), ((), ())), preferred_element_type=jnp.float32
    )
    return (mixed, weight_grad)


def solution(mesh):
    placed = (
        P("chan", "seq"),
        P("chan"),
        P("chan", None),
        P("chan", "seq"),
        P("chan"),
        P("chan", "seq"),
        P(None, "seq"),
    )
    return jax.shard_map(
        shards,
        mesh=mesh,
        in_specs=placed,
        out_specs=(P("chan", "seq"), P("seq", "chan")),
        check_vma=False,
    )
```

profile of v0, /device:TPU:0, one launch (start us, length us, event | category | flops | bytes accessed | tf_op | source)
XLA Modules:
  0.0 184.4 jit_solution(16678184828693716588)
XLA Ops:
  7.2 0.0 copy-start.2
  7.2 1.3 fusion.43
  8.4 13.5 %psum.7 = f32[256]{0:T(256)S(1)} all-reduce(f32[256]{0:T(256)S(1)} %fusion.43), channel_id=1, replica_groups=mesh['seq'=8,'chan'=4] {'chan'}, use_global_device_ids=true, to_apply=%region_1.0 | all-reduce | flops 256 | bytes 2048 | tf_op jit(solution)/shard_map/psum | solution.py:117
  21.9 1.2 fusion.45
  23.2 1.3 collective-permute-start
  24.5 4.6 %all-to-all-start.1 = ((bf16[8,128,256]{2,1,0:T(8,128)(2,1)}), bf16[8,128,256]{2,1,0:T(8,128)(2,1)S(1)}, u32[]{:S(2)}, u32[]{:S(2)}) async-start(bf16[8,128,256]{2,1,0:T(8,128)(2,1)} %bitcast.13), calls=%async_computation.1 | async-start | bytes 1048576 | tf_op jit(solution)/shard_map/all_to_all | solution.py:133
  29.1 0.1 multiply_cosine_fusion.3
  29.3 0.0 copy-done.2
  29.3 0.7 rev.3
  30.0 1.0 copy.57
  31.1 0.1 copy.62
  31.1 0.1 multiply_sine_fusion.3
  31.3 0.1 copy.65
  31.4 0.8 dynamic_slice.3
  32.1 0.1 multiply_sine_fusion
  32.3 0.0 collective-permute-done
  32.3 0.1 slice.9
  32.4 0.4 maximum_bitcast_fusion
  32.8 2.2 %copy.56 = bf16[1,1024,383]{1,0,2:T(2,128)(2,1)S(1)} copy(bf16[1,1024,383]{2,1,0:T(8,128)(2,1)S(1)} %maximum_bitcast_fusion) | data formatting | bytes 1568768 | tf_op jit(solution)/shard_map/broadcast_in_dim | solution.py:20
  35.1 12.7 %convolution_convert_fusion = bf16[1,1024,256]{1,0,2:T(2,128)(2,1)S(1)} fusion(bf16[1,1024,383]{1,0,2:T(2,128)(2,1)S(1)} %copy.56, f32[1024,1,128]{0,1,2:T(1,128)} %copy.57), kind=kOutput, calls=%fused_computation.43 | convolution fusion | flops 402915328 | bytes 1832960 | tf_op jit(solution)/shard_map/conv_general_dilated | solution.py:19
  47.8 2.0 %copy.58 = bf16[1,1024,256]{2,1,0:T(8,128)(2,1)} copy(bf16[1,1024,256]{1,0,2:T(2,128)(2,1)S(1)} %convolution_convert_fusion) | data formatting | bytes 1048576 | tf_op jit(solution)/shard_map/convert_element_type | solution.py:130
  49.8 0.0 all-to-all-done.1
  49.8 4.2 %all-to-all-start = ((bf16[8,128,256]{2,1,0:T(8,128)(2,1)}), bf16[8,128,256]{2,1,0:T(8,128)(2,1)S(1)}, u32[]{:S(2)}, u32[]{:S(2)}) async-start(bf16[8,128,256]{2,1,0:T(8,128)(2,1)} %bitcast.2), calls=%async_computation | async-start | bytes 1048576 | tf_op jit(solution)/shard_map/all_to_all | solution.py:132
  54.0 0.2 all-gather.2.cloned.1.call-start
  54.2 0.3 copy.68
  54.5 0.6 fusion.48
  55.1 0.6 fusion.51
  55.6 0.6 convolution_add_fusion.1
  56.2 1.6 subtract_bitcast_fusion
  57.8 3.3 %fusion.6 = f32[128,64,64]{0,2,1:T(8,128)S(1)} fusion(f32[128,64,64]{0,1,2:T(8,128)S(1)} %get-tuple-element.13), kind=kOutput, calls=%fused_computation.16 | convolution fusion | flops 402710528 | bytes 4194304 | tf_op jit(solution)/shard_map/ckm,jm->ckj/dot_general | solution.py:42
  61.2 3.4 %fusion.31 = f32[128,64,64]{0,2,1:T(8,128)S(1)} fusion(f32[128,64,64]{0,2,1:T(8,128)S(1)} %fusion.6, f32[128,64,64]{0,1,2:T(8,128)S(1)} %get-tuple-element.12), kind=kOutput, calls=%fused_computation.35 | convolution fusion | flops 403234816 | bytes 6291456 | tf_op jit(solution)/shard_map/ckm,jm->ckj/dot_general | solution.py:42
  64.6 3.6 %fusion.8 = f32[128,64,64]{0,2,1:T(8,128)S(1)} fusion(f32[128,64,64]{0,1,2:T(8,128)S(1)} %get-tuple-element.13), kind=kOutput, calls=%fused_computation.18 | convolution fusion | flops 402710528 | bytes 4194304 | tf_op jit(solution)/shard_map/ckm,jm->ckj/dot_general | solution.py:42
  68.1 4.7 %fusion.28 = f32[128,64,64]{0,2,1:T(8,128)} fusion(f32[128,64,64]{0,2,1:T(8,128)S(1)} %fusion.8, f32[128,64,64]{0,1,2:T(8,128)S(1)} %get-tuple-element.12), kind=kOutput, calls=%fused_computation.34 | convolution fusion | flops 403234816 | bytes 6291456 | tf_op jit(solution)/shard_map/ckm,jm->ckj/dot_general | solution.py:42
  72.9 0.0 all-to-all-done
  72.9 0.3 copy.59
  73.1 0.6 fusion.57
  73.7 0.6 fusion.54
  74.3 0.6 convolution_add_fusion.4
  74.9 1.6 fusion
  76.5 3.3 %fusion.16 = f32[128,64,64]{0,2,1:T(8,128)S(1)} fusion(f32[128,64,64]{0,1,2:T(8,128)S(1)} %get-tuple-element.15), kind=kOutput, calls=%fused_computation.26 | convolution fusion | flops 402710528 | bytes 4194304 | tf_op jit(solution)/shard_map/ckm,jm->ckj/dot_general | solution.py:42
  79.8 3.7 %fusion.14 = f32[128,64,64]{0,2,1:T(8,128)S(1)} fusion(f32[128,64,64]{0,1,2:T(8,128)S(1)} %get-tuple-element.15), kind=kOutput, calls=%fused_computation.24 | convolution fusion | flops 402710528 | bytes 4194304 | tf_op jit(solution)/shard_map/ckm,jm->ckj/dot_general | solution.py:42
  83.5 0.0 copy-start
  83.5 3.3 %fusion.22 = f32[128,64,64]{0,2,1:T(8,128)S(1)} fusion(f32[128,64,64]{0,2,1:T(8,128)S(1)} %fusion.16, f32[128,64,64]{0,1,2:T(8,128)S(1)} %get-tuple-element.14), kind=kOutput, calls=%fused_computation.32 | convolution fusion | flops 403234816 | bytes 6291456 | tf_op jit(solution)/shard_map/ckm,jm->ckj/dot_general | solution.py:42
  86.8 0.0 copy-done
  86.8 4.0 %multiply_add_fusion.1 = (f32[128,64,64]{0,2,1:T(8,128)S(1)}, f32[128,64,64]{0,2,1:T(8,128)S(1)}) fusion(f32[128,64,64]{0,2,1:T(8,128)S(1)} %copy-done, f32[128,64,64]{0,2,1:T(8,128)S(1)} %fusion.22, f32[128,64,64]{0,2,1:T(8,128)S(1)} %fusion.31, f32[128,64,64]{0,2,1:T(8,128)S(1)} %fusion.14, f32[128,64,64]{0,1,2:T(8,128)S(1)} %get-tuple-element.14), kind=kOutput, calls=%fused_computation.12 | convolution fusion | flops 406380544 | bytes 14680064 | tf_op jit(solution)/shard_map/ckm,jm->ckj/dot_general | solution.py:42
  90.8 2.2 %fusion.65 = f32[128,64,64]{0,2,1:T(8,128)S(1)} fusion(f32[128,64,64]{0,2,1:T(8,128)S(1)} %get-tuple-element.9), kind=kOutput, calls=%fused_computation.79 | convolution fusion | flops 402710528 | bytes 4194304 | tf_op jit(solution)/shard_map/ckj,mj->ckm/dot_general | solution.py:42
  93.0 2.3 %fusion.61 = f32[128,64,64]{0,2,1:T(8,128)S(1)} fusion(f32[128,64,64]{0,2,1:T(8,128)S(1)} %get-tuple-element.9), kind=kOutput, calls=%fused_computation.75 | convolution fusion | flops 402710528 | bytes 4194304 | tf_op jit(solution)/shard_map/ckj,mj->ckm/dot_general | solution.py:42
  95.3 2.2 %convolution_subtract_fusion = f32[128,64,64]{0,2,1:T(8,128)S(1)} fusion(f32[128,64,64]{0,2,1:T(8,128)S(1)} %fusion.65, f32[128,64,64]{0,2,1:T(8,128)S(1)} %get-tuple-element.8), kind=kOutput, calls=%fused_computation.38 | convolution fusion | flops 403234816 | bytes 6291456 | tf_op jit(solution)/shard_map/ckj,mj->ckm/dot_general | solution.py:42
  97.5 3.2 %multiply_subtract_fusion = (f32[128,64,64]{0,2,1:T(8,128)S(1)}, f32[128,64,64]{0,2,1:T(8,128)S(1)}) fusion(f32[128,64,64]{0,2,1:T(8,128)S(1)} %convolution_subtract_fusion, f32[64,64]{1,0:T(8,128)S(1)} %get-tuple-element.16, f32[64,64]{1,0:T(8,128)S(1)} %get-tuple-element.17, f32[128,64,64]{0,2,1:T(8,128)S(1)} %fusion.61, ...), kind=kOutput, calls=%fused_computation.11 | convolution fusion | flops 406380544 | bytes 10518528 | tf_op jit(solution)/shard_map/ckj,mj->ckm/dot_general | solution.py:42
  100.7 2.5 %fusion.2 = f32[128,64,32]{0,2,1:T(8,128)S(1)} fusion(f32[128,64,64]{0,2,1:T(8,128)S(1)} %get-tuple-element.11), kind=kOutput, calls=%fused_computation.6 | convolution fusion | flops 201355264 | bytes 3145728 | tf_op jit(solution)/shard_map/nk,ckm->cnm/dot_general | solution.py:42
  103.2 2.5 %fusion.40 = f32[128,32,64]{0,1,2:T(8,128)S(1)} fusion(f32[128,64,32]{0,2,1:T(8,128)S(1)} %fusion.2, f32[128,64,64]{0,2,1:T(8,128)S(1)} %get-tuple-element.10), kind=kOutput, calls=%fused_computation.46 | convolution fusion | flops 201879552 | bytes 4194304 | tf_op jit(solution)/shard_map/nk,ckm->cnm/dot_general | solution.py:42
  105.7 0.8 copy.83
  106.5 0.3 copy.84
  106.9 0.0 copy-start.1
  106.9 0.2 add_convert_fusion
  107.1 13.7 %all_to_all.58 = bf16[128,8,256]{2,0,1:T(8,128)(2,1)S(1)} all-to-all(bf16[128,8,256]{2,0,1:T(8,128)(2,1)S(1)} %add_convert_fusion), channel_id=1, replica_groups=mesh['seq'=8,'chan'=4] {'seq'}, dimensions={1} | all-to-all | bytes 1048576 | tf_op jit(solution)/shard_map/all_to_all | solution.py:139
  120.8 0.0 copy-done.1
  120.8 0.9 fusion.46
  121.7 0.0 all-gather.2.cloned.1.call-update
  121.7 38.7 %all_to_all.59 = bf16[8,512,256]{2,1,0:T(8,128)(2,1)S(1)} all-to-all(bf16[8,512,256]{2,1,0:T(8,128)(2,1)} %bitcast.121), channel_id=1, replica_groups=mesh['seq'=8,'chan'=4] {'seq'}, dimensions={0} | all-to-all | bytes 4194304 | tf_op jit(solution)/shard_map/all_to_all | solution.py:142
  160.4 2.4 %copy.85 = bf16[512,8,256]{0,2,1:T(8,128)(2,1)} copy(bf16[512,8,256]{2,0,1:T(8,128)(2,1)S(1)} %bitcast.118) | data formatting | bytes 4194304 | tf_op jit(solution)/shard_map/all_to_all | solution.py:142
  162.8 7.5 %all-gather.2.cloned.1.call-done = bf16[1024,2048]{1,0:T(8,128)(2,1)} async-done(((bf16[1024,256]{1,0:T(8,128)(2,1)}), bf16[1024,2048]{1,0:T(8,128)(2,1)}) %all-gather.2.cloned.1.call-update) | async-done | bytes 4194320 | tf_op jit(solution)/shard_map/all_gather | solution.py:141
  170.3 5.2 %convolution_bitcast_fusion = f32[512,1024]{0,1:T(8,128)S(1)} fusion(bf16[1024,2048]{1,0:T(8,128)(2,1)} %all-gather.2.cloned.1.call-done, bf16[512,2048]{0,1:T(8,128)(2,1)} %bitcast.122), kind=kOutput, calls=%fused_computation.36 | convolution fusion | flops 2147483648 | bytes 8388608 | tf_op jit(solution)/shard_map/dot_general | solution.py:143
  175.5 1.8 copy.86
  (2 shorter events, 0.0 us)
Async XLA Ops:
  7.2 22.1 %copy-start.2 = (f32[1024,128]{1,0:T(8,128)S(1)}, f32[1024,128]{1,0:T(8,128)}, u32[]{:S(2)}) copy-start(f32[1024,128]{1,0:T(8,128)} %param.9) | copy-start | bytes 1572868
  23.2 9.1 %collective-permute-start = (bf16[1024,128]{1,0:T(8,128)(2,1)S(1)}, bf16[1024,128]{1,0:T(8,128)(2,1)S(1)}, u32[]{:S(2)}, u32[]{:S(2)}) collective-permute-start(bf16[1024,128]{1,0:T(8,128)(2,1)S(1)} %slice.8), channel_id=1, source_target_pairs={{0,4},{4,8},{8,12},{12,16},{16,20},{20,24},{24,28},{1,5},{5,9},{9,... | collective-permute-start | bytes 786440 | tf_op jit(solution)/shard_map/ppermute | solution.py:14
  24.5 25.3 %all-to-all-start.1 = ((bf16[8,128,256]{2,1,0:T(8,128)(2,1)}), bf16[8,128,256]{2,1,0:T(8,128)(2,1)S(1)}, u32[]{:S(2)}, u32[]{:S(2)}) async-start(bf16[8,128,256]{2,1,0:T(8,128)(2,1)} %bitcast.13), calls=%async_computation.1 | async-start | bytes 1048576 | tf_op jit(solution)/shard_map/all_to_all | solution.py:133
  49.8 23.1 %all-to-all-start = ((bf16[8,128,256]{2,1,0:T(8,128)(2,1)}), bf16[8,128,256]{2,1,0:T(8,128)(2,1)S(1)}, u32[]{:S(2)}, u32[]{:S(2)}) async-start(bf16[8,128,256]{2,1,0:T(8,128)(2,1)} %bitcast.2), calls=%async_computation | async-start | bytes 1048576 | tf_op jit(solution)/shard_map/all_to_all | solution.py:132
  54.0 116.3 %all-gather.2.cloned.1.call-start = ((), (), s32[]{:S(2)}) async-start(), calls=%async_computation.4 | async-start | bytes 4718592 | tf_op jit(solution)/shard_map/all_gather | solution.py:141
  83.5 3.3 %copy-start = (f32[128,64,64]{0,2,1:T(8,128)S(1)}, f32[128,64,64]{0,2,1:T(8,128)}, u32[]{:S(2)}) copy-start(f32[128,64,64]{0,2,1:T(8,128)} %fusion.28) | copy-start | bytes 6291460
  106.9 13.9 %copy-start.1 = (bf16[1024,256]{1,0:T(8,128)(2,1)S(1)}, bf16[1024,256]{1,0:T(8,128)(2,1)}, u32[]{:S(2)}) copy-start(bf16[1024,256]{1,0:T(8,128)(2,1)} %param.12) | copy-start | bytes 1572868
Sparse Core Ops, SparseCore 0:
  121.8 48.4 all-gather.1
where the time goes:
time: 188 us; the launch traced here: 184 us
  matrix products  68.7 us (37%)
  blocking collectives  65.9 us (35%)
  between operations  14.6 us (8%)
  local copies, waits for them, and re-layouts  13 us (7%)
  starting transfers between devices  10.3 us (5%)
  waiting for transfers between devices  7.52 us (4%)
  other arithmetic  4.45 us (2%)
    dot_general x14, matrix products, product_einsum(): return jnp.einsum(form, left, right, precision=lax.Precision.HIGHEST)  44.1 us
    all_to_all x1, blocking collectives, shards(): lax.all_to_all(upstream, 'seq', split_axis=0, concat_axis=1, tiled=True)  38.7 us
    all_to_all x1, blocking collectives, shards(): lax.all_to_all(long_whole, 'seq', split_axis=1, concat_axis=0, tiled=True)  13.7 us
    psum x1, blocking collectives, shards(): squares = lax.psum(partial_squares, 'chan')  13.5 us
    conv_general_dilated x1, matrix products, short_conv(): lax.conv_general_dilated(padded[None], kernel, (1,), 'VALID', dimension_n...  12.7 us
    all_gather x1, waiting for transfers between devices, shards(): mixed_whole = lax.all_gather(mixed, 'seq', axis=1, tiled=True)  7.5 us
    dot_general x1, matrix products, shards(): lax.dot_general(owned, mixed_whole, (((1,), (1,)), ((), ())), preferred_e...  5.18 us
    all_to_all x1, starting transfers between devices, shards(): lax.all_to_all(long_filter, 'seq', split_axis=0, concat_axis=1, tiled=True)  4.62 us
  transfers between devices with their start and end apart: 4, of which 1 were waited for; matrix products, arithmetic and copies ran while one was open for 23% of the time, Pallas kernels for 0%

commit v1 on v0

--- a/solution.py
+++ b/solution.py
@@ -136,7 +136,10 @@
     long_whole = (long_conv + bias_slice[:, None] * short_whole.astype(jnp.float32)).astype(
         jnp.bfloat16
     )
-    long_out = lax.all_to_all(long_whole, "seq", split_axis=1, concat_axis=0, tiled=True)
+    long_out = jnp.concatenate(
+        lax.all_to_all(jnp.stack(jnp.split(long_whole, lax.axis_size("seq"), axis=1)), "seq", 0, 0),
+        axis=0,
+    )
     mixed = (gate_stream.astype(jnp.float32) * long_out.astype(jnp.float32)).astype(jnp.bfloat16)
     mixed_whole = lax.all_gather(mixed, "seq", axis=1, tiled=True)
     owned = lax.all_to_all(upstream, "seq", split_axis=0, concat_axis=1, tiled=True)

time: 188 us -> 191 us (1.016)
  transfers between devices with their start and end apart: 4 -> 4, of which waited for: 1 -> 1; matrix products, arithmetic and copies ran while one was open for 23% -> 22% of each run, Pallas kernels for 0% -> 0%
where the time goes in v1:
time: 191 us; the launch traced here: 187 us
  matrix products  68.7 us (36%)
  blocking collectives  65.9 us (35%)
  between operations  14.6 us (8%)
  local copies, waits for them, and re-layouts  14.5 us (8%)
  starting transfers between devices  10.3 us (5%)
  waiting for transfers between devices  7.52 us (4%)
  other arithmetic  5.44 us (3%)
    dot_general x14, matrix products, product_einsum(): return jnp.einsum(form, left, right, precision=lax.Precision.HIGHEST)  44.1 us
    all_to_all x1, blocking collectives, shards(): lax.all_to_all(upstream, 'seq', split_axis=0, concat_axis=1, tiled=True)  38.7 us
    all_to_all x1, blocking collectives, shards(): lax.all_to_all(jnp.stack(jnp.split(long_whole, lax.axis_size('seq'), axis...  13.7 us
    psum x1, blocking collectives, shards(): squares = lax.psum(partial_squares, 'chan')  13.5 us
    conv_general_dilated x1, matrix products, short_conv(): lax.conv_general_dilated(padded[None], kernel, (1,), 'VALID', dimension_n...  12.7 us
    all_gather x1, waiting for transfers between devices, shards(): mixed_whole = lax.all_gather(mixed, 'seq', axis=1, tiled=True)  7.5 us
    dot_general x1, matrix products, shards(): lax.dot_general(owned, mixed_whole, (((1,), (1,)), ((), ())), preferred_e...  5.18 us
    all_to_all x1, starting transfers between devices, shards(): lax.all_to_all(long_filter, 'seq', split_axis=0, concat_axis=1, tiled=True)  4.62 us
  transfers between devices with their start and end apart: 4, of which 1 were waited for; matrix products, arithmetic and copies ran while one was open for 22% of the time, Pallas kernels for 0%

profile of v1, /device:TPU:0, one launch (start us, length us, event | category | flops | bytes accessed | tf_op | source)
XLA Modules:
  0.0 187.0 jit_solution(1553224910816575011)
XLA Ops:
  7.2 1.3 fusion.43
  8.4 13.5 %psum.7 = f32[256]{0:T(256)S(1)} all-reduce(f32[256]{0:T(256)S(1)} %fusion.43), channel_id=1, replica_groups=mesh['seq'=8,'chan'=4] {'chan'}, use_global_device_ids=true, to_apply=%region_1.0 | all-reduce | flops 256 | bytes 2048 | tf_op jit(solution)/shard_map/psum | solution.py:117
  21.9 1.2 fusion.45
  23.2 1.3 collective-permute-start
  24.5 4.6 %all-to-all-start.1 = ((bf16[8,128,256]{2,1,0:T(8,128)(2,1)}), bf16[8,128,256]{2,1,0:T(8,128)(2,1)S(1)}, u32[]{:S(2)}, u32[]{:S(2)}) async-start(bf16[8,128,256]{2,1,0:T(8,128)(2,1)} %bitcast.13), calls=%async_computation.1 | async-start | bytes 1048576 | tf_op jit(solution)/shard_map/all_to_all | solution.py:133
  29.1 0.1 multiply_cosine_fusion.3
  29.3 0.0 copy-done.1
  29.3 0.7 rev.3
  30.0 1.0 copy.56
  31.1 0.1 copy.61
  31.1 0.1 multiply_sine_fusion.3
  31.3 0.1 copy.64
  31.4 0.8 dynamic_slice.3
  32.1 0.1 multiply_sine_fusion
  32.3 0.0 collective-permute-done
  32.3 0.1 slice.9
  32.4 0.4 maximum_bitcast_fusion
  32.8 2.2 %copy.55 = bf16[1,1024,383]{1,0,2:T(2,128)(2,1)S(1)} copy(bf16[1,1024,383]{2,1,0:T(8,128)(2,1)S(1)} %maximum_bitcast_fusion) | data formatting | bytes 1568768 | tf_op jit(solution)/shard_map/broadcast_in_dim | solution.py:20
  35.1 12.7 %convolution_convert_fusion = bf16[1,1024,256]{1,0,2:T(2,128)(2,1)S(1)} fusion(bf16[1,1024,383]{1,0,2:T(2,128)(2,1)S(1)} %copy.55, f32[1024,1,128]{0,1,2:T(1,128)} %copy.56), kind=kOutput, calls=%fused_computation.43 | convolution fusion | flops 402915328 | bytes 1832960 | tf_op jit(solution)/shard_map/conv_general_dilated | solution.py:19
  47.8 2.0 %copy.57 = bf16[1,1024,256]{2,1,0:T(8,128)(2,1)} copy(bf16[1,1024,256]{1,0,2:T(2,128)(2,1)S(1)} %convolution_convert_fusion) | data formatting | bytes 1048576 | tf_op jit(solution)/shard_map/convert_element_type | solution.py:130
  49.8 0.0 all-to-all-done.1
  49.8 4.2 %all-to-all-start = ((bf16[8,128,256]{2,1,0:T(8,128)(2,1)}), bf16[8,128,256]{2,1,0:T(8,128)(2,1)S(1)}, u32[]{:S(2)}, u32[]{:S(2)}) async-start(bf16[8,128,256]{2,1,0:T(8,128)(2,1)} %bitcast.2), calls=%async_computation | async-start | bytes 1048576 | tf_op jit(solution)/shard_map/all_to_all | solution.py:132
  54.0 0.2 all-gather.2.cloned.1.call-start
  54.2 0.3 copy.67
  54.5 0.6 fusion.50
  55.1 0.6 fusion.53
  55.6 0.6 convolution_add_fusion.1
  56.2 1.6 subtract_bitcast_fusion
  57.8 3.3 %fusion.6 = f32[128,64,64]{0,2,1:T(8,128)S(1)} fusion(f32[128,64,64]{0,1,2:T(8,128)S(1)} %get-tuple-element.13), kind=kOutput, calls=%fused_computation.16 | convolution fusion | flops 402710528 | bytes 4194304 | tf_op jit(solution)/shard_map/ckm,jm->ckj/dot_general | solution.py:42
  61.2 3.4 %fusion.31 = f32[128,64,64]{0,2,1:T(8,128)S(1)} fusion(f32[128,64,64]{0,2,1:T(8,128)S(1)} %fusion.6, f32[128,64,64]{0,1,2:T(8,128)S(1)} %get-tuple-element.12), kind=kOutput, calls=%fused_computation.35 | convolution fusion | flops 403234816 | bytes 6291456 | tf_op jit(solution)/shard_map/ckm,jm->ckj/dot_general | solution.py:42
  64.6 3.6 %fusion.8 = f32[128,64,64]{0,2,1:T(8,128)S(1)} fusion(f32[128,64,64]{0,1,2:T(8,128)S(1)} %get-tuple-element.13), kind=kOutput, calls=%fused_computation.18 | convolution fusion | flops 402710528 | bytes 4194304 | tf_op jit(solution)/shard_map/ckm,jm->ckj/dot_general | solution.py:42
  68.1 4.7 %fusion.28 = f32[128,64,64]{0,2,1:T(8,128)} fusion(f32[128,64,64]{0,2,1:T(8,128)S(1)} %fusion.8, f32[128,64,64]{0,1,2:T(8,128)S(1)} %get-tuple-element.12), kind=kOutput, calls=%fused_computation.34 | convolution fusion | flops 403234816 | bytes 6291456 | tf_op jit(solution)/shard_map/ckm,jm->ckj/dot_general | solution.py:42
  72.9 0.0 all-to-all-done
  72.9 0.3 copy.58
  73.1 0.6 fusion.59
  73.7 0.6 fusion.56
  74.3 0.6 convolution_add_fusion.4
  74.9 1.6 fusion
  76.5 3.3 %fusion.16 = f32[128,64,64]{0,2,1:T(8,128)S(1)} fusion(f32[128,64,64]{0,1,2:T(8,128)S(1)} %get-tuple-element.15), kind=kOutput, calls=%fused_computation.26 | convolution fusion | flops 402710528 | bytes 4194304 | tf_op jit(solution)/shard_map/ckm,jm->ckj/dot_general | solution.py:42
  79.8 3.7 %fusion.14 = f32[128,64,64]{0,2,1:T(8,128)S(1)} fusion(f32[128,64,64]{0,1,2:T(8,128)S(1)} %get-tuple-element.15), kind=kOutput, calls=%fused_computation.24 | convolution fusion | flops 402710528 | bytes 4194304 | tf_op jit(solution)/shard_map/ckm,jm->ckj/dot_general | solution.py:42
  83.5 0.0 copy-start
  83.5 3.3 %fusion.22 = f32[128,64,64]{0,2,1:T(8,128)S(1)} fusion(f32[128,64,64]{0,2,1:T(8,128)S(1)} %fusion.16, f32[128,64,64]{0,1,2:T(8,128)S(1)} %get-tuple-element.14), kind=kOutput, calls=%fused_computation.32 | convolution fusion | flops 403234816 | bytes 6291456 | tf_op jit(solution)/shard_map/ckm,jm->ckj/dot_general | solution.py:42
  86.8 4.0 %multiply_add_fusion.1 = (f32[128,64,64]{0,2,1:T(8,128)S(1)}, f32[128,64,64]{0,2,1:T(8,128)S(1)}) fusion(f32[128,64,64]{0,2,1:T(8,128)S(1)} %copy-done, f32[128,64,64]{0,2,1:T(8,128)S(1)} %fusion.22, f32[128,64,64]{0,2,1:T(8,128)S(1)} %fusion.31, f32[128,64,64]{0,2,1:T(8,128)S(1)} %fusion.14, f32[128,64,64]{0,1,2:T(8,128)S(1)} %get-tuple-element.14), kind=kOutput, calls=%fused_computation.12 | convolution fusion | flops 406380544 | bytes 14680064 | tf_op jit(solution)/shard_map/ckm,jm->ckj/dot_general | solution.py:42
  90.8 2.2 %fusion.75 = f32[128,64,64]{0,2,1:T(8,128)S(1)} fusion(f32[128,64,64]{0,2,1:T(8,128)S(1)} %get-tuple-element.9), kind=kOutput, calls=%fused_computation.97 | convolution fusion | flops 402710528 | bytes 4194304 | tf_op jit(solution)/shard_map/ckj,mj->ckm/dot_general | solution.py:42
  93.0 2.3 %fusion.71 = f32[128,64,64]{0,2,1:T(8,128)S(1)} fusion(f32[128,64,64]{0,2,1:T(8,128)S(1)} %get-tuple-element.9), kind=kOutput, calls=%fused_computation.93 | convolution fusion | flops 402710528 | bytes 4194304 | tf_op jit(solution)/shard_map/ckj,mj->ckm/dot_general | solution.py:42
  95.3 2.2 %convolution_subtract_fusion = f32[128,64,64]{0,2,1:T(8,128)S(1)} fusion(f32[128,64,64]{0,2,1:T(8,128)S(1)} %fusion.75, f32[128,64,64]{0,2,1:T(8,128)S(1)} %get-tuple-element.8), kind=kOutput, calls=%fused_computation.38 | convolution fusion | flops 403234816 | bytes 6291456 | tf_op jit(solution)/shard_map/ckj,mj->ckm/dot_general | solution.py:42
  97.5 3.2 %multiply_subtract_fusion = (f32[128,64,64]{0,2,1:T(8,128)S(1)}, f32[128,64,64]{0,2,1:T(8,128)S(1)}) fusion(f32[128,64,64]{0,2,1:T(8,128)S(1)} %convolution_subtract_fusion, f32[64,64]{1,0:T(8,128)S(1)} %get-tuple-element.16, f32[64,64]{1,0:T(8,128)S(1)} %get-tuple-element.17, f32[128,64,64]{0,2,1:T(8,128)S(1)} %fusion.71, ...), kind=kOutput, calls=%fused_computation.11 | convolution fusion | flops 406380544 | bytes 10518528 | tf_op jit(solution)/shard_map/ckj,mj->ckm/dot_general | solution.py:42
  100.7 2.5 %fusion.2 = f32[128,64,32]{0,2,1:T(8,128)S(1)} fusion(f32[128,64,64]{0,2,1:T(8,128)S(1)} %get-tuple-element.11), kind=kOutput, calls=%fused_computation.6 | convolution fusion | flops 201355264 | bytes 3145728 | tf_op jit(solution)/shard_map/nk,ckm->cnm/dot_general | solution.py:42
  103.2 2.5 %fusion.40 = f32[128,32,64]{0,1,2:T(8,128)S(1)} fusion(f32[128,64,32]{0,2,1:T(8,128)S(1)} %fusion.2, f32[128,64,64]{0,2,1:T(8,128)S(1)} %get-tuple-element.10), kind=kOutput, calls=%fused_computation.46 | convolution fusion | flops 201879552 | bytes 4194304 | tf_op jit(solution)/shard_map/nk,ckm->cnm/dot_general | solution.py:42
  105.7 0.8 copy.82
  106.5 1.1 bitcast_convert_fusion
  107.6 1.5 copy.83
  109.2 0.1 fusion.48
  109.3 0.0 copy-start.2
  109.5 13.7 %all_to_all.53 = bf16[8,128,256]{1,2,0:T(8,128)(2,1)S(1)} all-to-all(bf16[8,128,256]{1,2,0:T(8,128)(2,1)S(1)} %fusion.61), channel_id=1, replica_groups=mesh['seq'=8,'chan'=4] {'seq'}, dimensions={0} | all-to-all | bytes 1048576 | tf_op jit(solution)/shard_map/all_to_all | solution.py:140
  123.1 0.2 copy.84
  123.3 0.0 copy-done.2
  123.4 0.9 fusion.46
  124.3 0.0 all-gather.2.cloned.1.call-update
  124.3 38.7 %all_to_all.54 = bf16[8,512,256]{2,1,0:T(8,128)(2,1)S(1)} all-to-all(bf16[8,512,256]{2,1,0:T(8,128)(2,1)} %bitcast.157), channel_id=1, replica_groups=mesh['seq'=8,'chan'=4] {'seq'}, dimensions={0} | all-to-all | bytes 4194304 | tf_op jit(solution)/shard_map/all_to_all | solution.py:145
  163.0 2.4 %copy.85 = bf16[512,8,256]{0,2,1:T(8,128)(2,1)} copy(bf16[512,8,256]{2,0,1:T(8,128)(2,1)S(1)} %bitcast.155) | data formatting | bytes 4194304 | tf_op jit(solution)/shard_map/all_to_all | solution.py:145
  165.4 7.5 %all-gather.2.cloned.1.call-done = bf16[1024,2048]{1,0:T(8,128)(2,1)} async-done(((bf16[1024,256]{1,0:T(8,128)(2,1)}), bf16[1024,2048]{1,0:T(8,128)(2,1)}) %all-gather.2.cloned.1.call-update) | async-done | bytes 4194320 | tf_op jit(solution)/shard_map/all_gather | solution.py:144
  172.9 5.2 %convolution_bitcast_fusion = f32[512,1024]{0,1:T(8,128)S(1)} fusion(bf16[1024,2048]{1,0:T(8,128)(2,1)} %all-gather.2.cloned.1.call-done, bf16[512,2048]{0,1:T(8,128)(2,1)} %bitcast.158), kind=kOutput, calls=%fused_computation.36 | convolution fusion | flops 2147483648 | bytes 8388608 | tf_op jit(solution)/shard_map/dot_general | solution.py:146
  178.1 1.8 copy.86
  (12 shorter events, 0.1 us)
Async XLA Ops:
  7.2 22.1 %copy-start.1 = (f32[1024,128]{1,0:T(8,128)S(1)}, f32[1024,128]{1,0:T(8,128)}, u32[]{:S(2)}) copy-start(f32[1024,128]{1,0:T(8,128)} %param.9) | copy-start | bytes 1572868
  23.2 9.1 %collective-permute-start = (bf16[1024,128]{1,0:T(8,128)(2,1)S(1)}, bf16[1024,128]{1,0:T(8,128)(2,1)S(1)}, u32[]{:S(2)}, u32[]{:S(2)}) collective-permute-start(bf16[1024,128]{1,0:T(8,128)(2,1)S(1)} %slice.8), channel_id=1, source_target_pairs={{0,4},{4,8},{8,12},{12,16},{16,20},{20,24},{24,28},{1,5},{5,9},{9,... | collective-permute-start | bytes 786440 | tf_op jit(solution)/shard_map/ppermute | solution.py:14
  24.5 25.3 %all-to-all-start.1 = ((bf16[8,128,256]{2,1,0:T(8,128)(2,1)}), bf16[8,128,256]{2,1,0:T(8,128)(2,1)S(1)}, u32[]{:S(2)}, u32[]{:S(2)}) async-start(bf16[8,128,256]{2,1,0:T(8,128)(2,1)} %bitcast.13), calls=%async_computation.1 | async-start | bytes 1048576 | tf_op jit(solution)/shard_map/all_to_all | solution.py:133
  49.8 23.1 %all-to-all-start = ((bf16[8,128,256]{2,1,0:T(8,128)(2,1)}), bf16[8,128,256]{2,1,0:T(8,128)(2,1)S(1)}, u32[]{:S(2)}, u32[]{:S(2)}) async-start(bf16[8,128,256]{2,1,0:T(8,128)(2,1)} %bitcast.2), calls=%async_computation | async-start | bytes 1048576 | tf_op jit(solution)/shard_map/all_to_all | solution.py:132
  54.0 118.9 %all-gather.2.cloned.1.call-start = ((), (), s32[]{:S(2)}) async-start(), calls=%async_computation.4 | async-start | bytes 4718592 | tf_op jit(solution)/shard_map/all_gather | solution.py:144
  83.5 3.3 %copy-start = (f32[128,64,64]{0,2,1:T(8,128)S(1)}, f32[128,64,64]{0,2,1:T(8,128)}, u32[]{:S(2)}) copy-start(f32[128,64,64]{0,2,1:T(8,128)} %fusion.28) | copy-start | bytes 6291460
  109.3 14.1 %copy-start.2 = (bf16[1024,256]{1,0:T(8,128)(2,1)S(1)}, bf16[1024,256]{1,0:T(8,128)(2,1)}, u32[]{:S(2)}) copy-start(bf16[1024,256]{1,0:T(8,128)(2,1)} %param.12) | copy-start | bytes 1572868
Sparse Core Ops, SparseCore 0:
  124.4 48.4 all-gather.1
